TPU v7x, 32 devices: a whole 2x2x4 slice. The times are simulated.
32 devices in a mesh: rep: 2 (over y), cell: 4 (over x, core), gene: 4 (over z).
Axes of the slice: x: 2, y: 2, z: 4, core: 2. Of those that a mesh axis runs over, the one named last changes fastest.
Arguments:
- counts: int32 [4096, 5120], P('cell', 'gene'), may hold values from 0 to 63
- usage_init: float32 [8192, 200], P(('rep', 'cell')), parts along dimension 0, may hold values from 0.05 to 1
- program_init: float32 [400, 5120], P('rep', 'gene'), parts along dimension 0, may hold values from 0.05 to 1
Outputs:
- usage: float32 [8192, 200], P(('rep', 'cell')), parts along dimension 0
- program: float32 [400, 5120], P('rep', 'gene'), parts along dimension 0
There are 2 independent parts, one for each index of `rep`. A program takes and returns all parts, laid end to end along the dimension named above; an argument that names none is the same for every part. Nothing has to cross between parts.
All inputs are finite; a program needn't handle non-finite values.
Results may differ from a plain program's by a relative error of at most 0.0001.
Values sent between devices are 32-bit elements; how exact they have to be, the bound alone decides.
A program may use at most 64 MiB of HBM per device.

v0:
```python
import functools

import jax
import jax.numpy as jnp
from jax import lax
from jax.experimental import pallas as pl
from jax.experimental.pallas import tpu as pltpu
from jax.sharding import PartitionSpec as P

ITERS = 2
LANES = 128
WIDE = 2 * LANES
HOP = 4
GRAM_LAG, CORE_LAG, CHIP_LAG, SHARE_LAG = 3, 2, 6, 9

MESH = pl.DeviceIdType.MESH
f32 = jnp.float32


def dot(left, right, left_dim, right_dim):
    return lax.dot_general(
        left,
        right,
        (((left_dim,), (right_dim,)), ((), ())),
        preferred_element_type=f32,
    )


def parts(x):
    high = x.astype(jnp.bfloat16)
    return high, (x - high.astype(f32)).astype(jnp.bfloat16)


def dot_exact_right(left, right, right_dim):
    rows = left.shape[0]
    both = dot(jnp.concatenate(parts(left), 0), right, 1, right_dim)
    return both[:rows] + both[rows:]


def dot_three(left, right, right_dim):
    rows = left.shape[0]
    left_high, left_low = parts(left)
    right_high, right_low = parts(right)
    both = dot(jnp.concatenate([left_high, left_low], 0), right_high, 1, right_dim)
    return both[:rows] + (both[rows:] + dot(left_high, right_low, 1, right_dim))


def gram_blocks(n, rows):
    return [(r, 0) for r in range(n)] + [(r, 1) for r in range(n) if (r + 1) * rows > LANES]


def kernel(
    sizes,
    counts_ref, u_ref, p_ref, u_out, p_out,
    counts, e_ref,
    u_buf, p_buf, zp, z_in, z_out, z_mid, z_fin, g_own, g_all, gram,
    c_send, c_in, x_buf, x_fin, u_gram,
    zs_sem, zr_sem, gs_sem, gr_sem, cs_sem, cr_sem, xs_sem, xr_sem, fs_sem, fr_sem, in_sem,
):
    n_gene, n_cell, n, rows, cells, genes, real_genes, n_slots = sizes
    k = n * rows
    n_chip, reach = n_cell // 2, n_gene // 2
    subs = cells // WIDE
    half_genes = genes // 2
    blocks = gram_blocks(n, rows)
    lead = 2 * subs
    n_pieces = n * subs + n_slots

    z = lax.axis_index("gene")
    cell = lax.axis_index("cell")
    core = lax.rem(cell, 2)
    chip = cell // 2
    other = 1 - core
    low = z < reach
    far = jnp.where(low, reach - 1 - z, z - reach)
    inner = jnp.where(low, z + 1, z - 1)
    outer = jnp.where(low, z - 1, z + 1)
    middle, edge = far == 0, far == reach - 1

    def load(s):
        at_row = pl.ds(pl.multiple_of(s * WIDE, WIDE), WIDE)
        return pltpu.make_async_copy(counts_ref.at[at_row], counts.at[s], in_sem.at[s])

    for s in range(subs):
        load(s).start()

    barrier = pltpu.get_barrier_semaphore()
    pl.semaphore_signal(barrier, inc=1, device_id={"gene": inner}, device_id_type=MESH)

    @pl.when(jnp.logical_not(edge))
    def _():
        pl.semaphore_signal(barrier, inc=1, device_id={"gene": outer}, device_id_type=MESH)

    for away in range(1, n_cell):
        peer = lax.rem(cell + away, n_cell)
        pl.semaphore_signal(barrier, inc=1, device_id={"cell": peer}, device_id_type=MESH)
    pl.semaphore_wait(barrier, n_cell + 1 - jnp.where(edge, 1, 0))

    u_buf[0] = u_ref[...]
    p_buf[0] = p_ref[...]

    def take_counts(s):
        load(s).wait()
        at_row = pl.ds(pl.multiple_of(s * WIDE, WIDE), WIDE)
        e_ref[at_row, :real_genes] = counts[s].astype(f32).astype(jnp.bfloat16)
        if real_genes < genes:
            e_ref[at_row, real_genes:] = jnp.zeros((WIDE, genes - real_genes), jnp.bfloat16)

    def remote(src, dst, send, recv, to):
        return pltpu.make_async_remote_copy(
            src_ref=src, dst_ref=dst, send_sem=send, recv_sem=recv, device_id=to, device_id_type=MESH
        )

    def inward(it, c):
        return remote(z_out.at[it, c], z_in.at[it, c], zs_sem.at[it, 0, c], zr_sem.at[it, 0, c], {"gene": inner})

    def across(it, c):
        return remote(z_out.at[it, c], z_mid.at[it, c], zs_sem.at[it, 0, c], zr_sem.at[it, 1, c], {"gene": inner})

    def outward(it, c):
        return remote(z_fin.at[it, c], z_fin.at[it, c], zs_sem.at[it, 1, c], zr_sem.at[it, 1, c], {"gene": outer})

    def spread(it, s, away):
        to = lax.rem(cell + away, n_cell)
        mine = g_all.at[it, s * n_cell + cell]
        return remote(mine, mine, gs_sem.at[it, s, away - 1], gr_sem.at[it, s, away - 1], {"cell": to})

    def spread_from(it, s, away):
        to = lax.rem(cell + n_cell - away, n_cell)
        theirs = g_all.at[it, s * n_cell + to]
        return remote(theirs, theirs, gs_sem.at[it, s, away - 1], gr_sem.at[it, s, away - 1], {"cell": to})

    def to_core(it, j):
        return remote(
            c_send.at[it, j, other], c_in.at[it, j], cs_sem.at[it, j], cr_sem.at[it, j], {"cell": chip * 2 + other}
        )

    def to_chip(it, j, away):
        to = lax.rem(chip + away, n_chip)
        mine = x_buf.at[it, j, chip]
        return remote(mine, mine, xs_sem.at[it, j, away - 1], xr_sem.at[it, j, away - 1], {"cell": to * 2 + core})

    def from_chip(it, j, away):
        to = lax.rem(chip + n_chip - away, n_chip)
        theirs = x_buf.at[it, j, to]
        return remote(theirs, theirs, xs_sem.at[it, j, away - 1], xr_sem.at[it, j, away - 1], {"cell": to * 2 + core})

    def share(it, j, which):
        piece = x_fin.at[it, j, which]
        return remote(piece, piece, fs_sem.at[it, j], fr_sem.at[it, j], {"cell": chip * 2 + other})

    def gather_in(it, c):
        @pl.when(edge)
        def _():
            z_out[it, c] = zp[c]

        @pl.when(jnp.logical_not(edge))
        def _():
            inward(it, c).wait_recv()
            z_out[it, c] = zp[c] + z_in[it, c]

        @pl.when(middle)
        def _():
            across(it, c).start()

        @pl.when(jnp.logical_not(middle))
        def _():
            inward(it, c).start()

    def spread_out(it, c):
        @pl.when(middle)
        def _():
            across(it, c).wait_recv()
            z_fin[it, c] = z_out[it, c] + z_mid[it, c]

        @pl.when(jnp.logical_not(middle))
        def _():
            outward(it, c).wait_recv()

        @pl.when(jnp.logical_not(edge))
        def _():
            outward(it, c).start()

    def numerator(it, q):
        j, s = q // subs, lax.rem(q, subs)
        at_row = pl.ds(pl.multiple_of(s * WIDE, WIDE), WIDE)
        zp[q + jnp.where(q >= lead, n_slots, 0)] = dot_exact_right(p_buf[it, j], e_ref[at_row, :], 1)

    def own_gram(it):
        whole = p_buf[it].reshape(k, genes)
        own = dot_three(whole, whole, 1)
        own = jnp.concatenate([own, jnp.zeros((k, 2 * LANES - k), f32)], 1)
        for i in range(2 * n_slots * n_cell):
            r, h = blocks[min(i, len(blocks) - 1)]
            at = (i % 2) * LANES
            g_own[i // 2, :, at:at + LANES] = own[r * rows:(r + 1) * rows, h * LANES:(h + 1) * LANES]
        for s in range(n_slots):
            zp[lead + s] = g_own[s * n_cell + cell]

    def spread_gram(it):
        for s in range(n_slots):
            g_all[it, s * n_cell + cell] = z_fin[it, lead + s]
            for away in range(1, n_cell):
                spread(it, s, away).start()

    def join_gram(it):
        for s in range(n_slots):
            for away in range(1, n_cell):
                spread_from(it, s, away).wait_recv()
        none = jnp.zeros((rows, LANES), f32)
        lines = []
        for r in range(n):
            halves = []
            for h in range(2):
                if (r, h) in blocks:
                    i = blocks.index((r, h))
                    halves.append(g_all[it, i // 2, :, (i % 2) * LANES:(i % 2 + 1) * LANES])
                else:
                    halves.append(none)
            lines.append(jnp.concatenate(halves, 1))
        lines.append(jnp.zeros((2 * LANES - k, 2 * LANES), f32))
        known = jnp.concatenate(lines, 0)
        first = min(r for r, h in blocks if h == 1) * rows
        row = lax.broadcasted_iota(jnp.int32, known.shape, 0)
        column = lax.broadcasted_iota(jnp.int32, known.shape, 1)
        missing = jnp.logical_and(row < first, column >= LANES)
        full = jnp.where(missing, known.T, known)
        for r in range(n):
            gram[r] = full[r * rows:(r + 1) * rows]

    def update_usage(it, j):
        first = j * subs + jnp.where(j >= 2, n_slots, 0)
        top = jnp.concatenate([z_fin[it, first + s] for s in range(subs)], 1)
        old = u_buf[it].reshape(k, cells)
        new = u_buf[it, j] * top / dot_three(gram[j][:, :k], old, 0)
        u_buf[it + 1, j] = new

        def half(h):
            at = pl.ds(pl.multiple_of(h * half_genes, LANES), half_genes)
            c_send[it, j, h, :, :half_genes] = dot_exact_right(new, e_ref[:, at], 0)

        own = dot_three(new, u_buf[it + 1].reshape(k, cells), 1)
        c_send[it, j, 0, :, half_genes:] = own[:, :LANES]
        c_send[it, j, 1, :, half_genes:] = jnp.concatenate(
            [own[:, LANES:], jnp.zeros((rows, 2 * LANES - k), f32)], 1
        )
        half(other)
        to_core(it, j).start()
        half(core)

    def update_program(it, j):
        top = jnp.concatenate([x_fin[it, j, h, :, :half_genes] for h in range(2)], 1)
        old = p_buf[it].reshape(k, genes)
        at_row = pl.ds(pl.multiple_of(j * rows, rows), rows)
        new = p_buf[it, j] * top / dot_three(u_gram[at_row, :][:, :k], old, 0)
        if real_genes < genes:
            inside = lax.broadcasted_iota(jnp.int32, (rows, genes), 1) < real_genes
            new = jnp.where(inside, new, 0.0)
        return new

    def settle_pieces(it):
        def pieces(c, carry):
            inward(it, c).wait_send()

            @pl.when(jnp.logical_not(edge))
            def _():
                outward(it, c).wait_send()

            return carry

        lax.fori_loop(0, n_pieces, pieces, 0)
        for s in range(n_slots):
            for away in range(1, n_cell):
                spread(it, s, away).wait_send()

    turns = [
        max((j + 1) * subs + (n_slots if j >= 2 else 0) - 1, lead + n_slots + GRAM_LAG + 2 * j) for j in range(n)
    ]
    program_turns = [j * lead // n for j in range(n)]

    def step(it, carry):
        u_buf[it + 1] = jnp.zeros(u_buf.shape[1:], f32)
        inward_lag = (reach - 1 - far) * HOP
        done = (reach + far) * HOP
        ticks = (2 * reach - 1) * HOP + turns[-1] + SHARE_LAG + 1

        def tick(t, carry):
            def at(lag, count, act):
                @pl.when(jnp.logical_and(t >= lag, t < lag + count))
                def _():
                    act(t - lag)

            def at_turn(since, when, act):
                hit, j = since == when[0], 0
                for i in range(1, n):
                    now = since == when[i]
                    hit, j = jnp.logical_or(hit, now), jnp.where(now, i, j)

                @pl.when(hit)
                def _():
                    act(j)

            def next_program(j):
                p_buf[it, j] = update_program(it - 1, j)

            @pl.when(jnp.logical_and(it == 0, t < subs))
            def _():
                take_counts(t)

            at_turn(jnp.where(it > 0, t, -1), program_turns, next_program)
            q = t - jnp.where(t >= lead + n_slots, n_slots, 0)
            a_piece = jnp.logical_and(jnp.logical_or(t < lead, t >= lead + n_slots), q < n * subs)

            @pl.when(a_piece)
            def _():
                numerator(it, q)

            @pl.when(t == lead)
            def _():
                own_gram(it)

            at(inward_lag, n_pieces, lambda c: gather_in(it, c))
            at(done, n_pieces, lambda c: spread_out(it, c))

            @pl.when(t == done + lead + n_slots - 1)
            def _():
                spread_gram(it)

            @pl.when(t == done + lead + n_slots + GRAM_LAG)
            def _():
                join_gram(it)

            at_turn(t - done, turns, lambda j: update_usage(it, j))

            def join_core(j):
                to_core(it, j).wait_recv()
                x_buf[it, j, chip] = c_send[it, j, core] + c_in[it, j]
                for away in range(1, n_chip):
                    to_chip(it, j, away).start()

            at_turn(t - done - CORE_LAG, turns, join_core)

            @pl.when(t == done + CORE_LAG + turns[-1])
            def _():
                settle_pieces(it)
            def join_chip(j):
                for away in range(1, n_chip):
                    from_chip(it, j, away).wait_recv()
                total = x_buf[it, j, 0]
                for peer in range(1, n_chip):
                    total = total + x_buf[it, j, peer]
                x_fin[it, j, core] = total
                share(it, j, core).start()

            at_turn(t - done - CHIP_LAG, turns, join_chip)
            at_turn(t - done - SHARE_LAG, turns, lambda j: share(it, j, other).wait_recv())
            return carry

        lax.fori_loop(0, ticks, tick, 0)

        columns = lax.broadcasted_iota(jnp.int32, (rows, 2 * LANES), 1)
        lower, strict = [], []
        for r in range(n):
            block = jnp.concatenate([x_fin[it, r, h, :, half_genes:] for h in range(2)], 1)
            lower.append(jnp.where(columns < (r + 1) * rows, block, 0.0))
            strict.append(jnp.where(columns < r * rows, block, 0.0))
        pad = jnp.zeros((2 * LANES - k, 2 * LANES), f32)
        u_gram[...] = jnp.concatenate(lower + [pad], 0) + jnp.concatenate(strict + [pad], 0).T
        return carry

    lax.fori_loop(0, ITERS, step, 0)

    def last_program(j, carry):
        p_out[j] = update_program(ITERS - 1, j)
        return carry

    lax.fori_loop(0, n, last_program, 0)
    u_out[...] = u_buf[ITERS]

    def settle(it, carry):
        def chunks(j, carry):
            to_core(it, j).wait_send()
            for away in range(1, n_chip):
                to_chip(it, j, away).wait_send()
            share(it, j, core).wait_send()
            return carry

        lax.fori_loop(0, n, chunks, 0)
        return carry

    lax.fori_loop(0, ITERS, settle, 0)


def body(mesh, counts, usage_init, program_init):
    cells, k = usage_init.shape
    real_genes = program_init.shape[1]
    n_gene, n_cell = mesh.shape["gene"], mesh.shape["cell"]
    n_chip = n_cell // 2
    rows = max(r for r in range(8, 41, 8) if k % r == 0)
    n = k // rows
    genes = -(-real_genes // (2 * LANES)) * 2 * LANES
    n_slots = -(-len(gram_blocks(n, rows)) // (2 * n_cell))
    n_pieces = n * (cells // WIDE) + n_slots
    width = genes // 2 + LANES

    program = program_init
    if genes > real_genes:
        program = jnp.pad(program, ((0, 0), (0, genes - real_genes)))

    sizes = (n_gene, n_cell, n, rows, cells, genes, real_genes, n_slots)
    vmem = pl.BlockSpec(memory_space=pltpu.VMEM)
    dma = pltpu.SemaphoreType.DMA
    usage, program = pl.pallas_call(
        functools.partial(kernel, sizes),
        out_shape=[
            jax.ShapeDtypeStruct((n, rows, cells), f32),
            jax.ShapeDtypeStruct((n, rows, genes), f32),
        ],
        in_specs=[pl.BlockSpec(memory_space=pl.ANY), vmem, vmem],
        out_specs=[vmem] * 2,
        scratch_shapes=[
            pltpu.VMEM((cells // WIDE, WIDE, real_genes), jnp.int32),
            pltpu.VMEM((cells, genes), jnp.bfloat16),
            pltpu.VMEM((ITERS + 1, n, rows, cells), f32),
            pltpu.VMEM((ITERS + 1, n, rows, genes), f32),
            pltpu.VMEM((n_pieces, rows, WIDE), f32),
            pltpu.VMEM((ITERS, n_pieces, rows, WIDE), f32),
            pltpu.VMEM((ITERS, n_pieces, rows, WIDE), f32),
            pltpu.VMEM((ITERS, n_pieces, rows, WIDE), f32),
            pltpu.VMEM((ITERS, n_pieces, rows, WIDE), f32),
            pltpu.VMEM((n_slots * n_cell, rows, WIDE), f32),
            pltpu.VMEM((ITERS, n_slots * n_cell, rows, WIDE), f32),
            pltpu.VMEM((n, rows, 2 * LANES), f32),
            pltpu.VMEM((ITERS, n, 2, rows, width), f32),
            pltpu.VMEM((ITERS, n, rows, width), f32),
            pltpu.VMEM((ITERS, n, n_chip, rows, width), f32),
            pltpu.VMEM((ITERS, n, 2, rows, width), f32),
            pltpu.VMEM((2 * LANES, 2 * LANES), f32),
            dma((ITERS, 2, n_pieces)),
            dma((ITERS, 2, n_pieces)),
            dma((ITERS, n_slots, n_cell - 1)),
            dma((ITERS, n_slots, n_cell - 1)),
            dma((ITERS, n)),
            dma((ITERS, n)),
            dma((ITERS, n, max(n_chip - 1, 1))),
            dma((ITERS, n, max(n_chip - 1, 1))),
            dma((ITERS, n)),
            dma((ITERS, n)),
            dma((cells // WIDE,)),
        ],
        compiler_params=pltpu.CompilerParams(
            collective_id=0, has_side_effects=True, vmem_limit_bytes=60 * 1024 * 1024
        ),
    )(
        counts,
        usage_init.T.reshape(n, rows, cells),
        program.reshape(n, rows, genes),
    )
    usage = usage.reshape(k, cells).T
    program = program.reshape(k, genes)[:, :real_genes]
    return usage, program


def solution(mesh):
    return jax.shard_map(
        functools.partial(body, mesh),
        mesh=mesh,
        in_specs=(P("cell", "gene"), P(("rep", "cell"), None), P("rep", "gene")),
        out_specs=(P(("rep", "cell"), None), P("rep", "gene")),
        check_vma=False,
    )
```

profile of v0, /device:TPU:0, one launch (start us, length us, event | category | flops | bytes accessed | tf_op | source)
XLA Modules:
  0.0 96.3 jit_solution(16855797750479203178)
XLA Ops:
  0.6 91.3 %shard_map.50 = (f32[5,40,1024]{2,1,0:T(8,128)}, f32[5,40,1280]{2,1,0:T(8,128)}) custom-call(s32[1024,1280]{1,0:T(8,128)} %counts_ref.1, f32[5,40,1024]{2,1,0:T(8,128)} %bitcast.11, f32[5,40,1280]{2,1,0:T(8,128)} %bitcast.9), custom_call_target="tpu_custom_call" | custom-call | tf_op jit(solution)/shard_map/pallas_call | solution.py:413
  91.9 2.1 %copy.7 = f32[1024,200]{0,1:T(8,128)} copy(f32[1024,200]{0,1:T(8,128)} %bitcast.10) | data formatting | bytes 1638400
  94.0 2.2 %copy.8 = f32[200,1280]{1,0:T(8,128)} copy(f32[200,1280]{1,0:T(8,128)} %bitcast.8) | data formatting | bytes 2048000
where the time goes:
time: 97 us; the launch traced here: 96.3 us
  Pallas kernels  91.3 us (94%)
  local copies, waits for them, and re-layouts  4.36 us (4%)
    pallas_call x1, Pallas kernels, body(): pl.pallas_call(functools.partial(kernel, sizes), out_shape=[jax.ShapeDtyp...  91.3 us
    unnamed x2, local copies, waits for them, and re-layouts  4.36 us

commit v1 on v0

--- a/solution.py
+++ b/solution.py
@@ -11,7 +11,7 @@
 LANES = 128
 WIDE = 2 * LANES
 HOP = 4
-GRAM_LAG, CORE_LAG, CHIP_LAG, SHARE_LAG = 3, 2, 6, 9
+GRAM_LAG, CORE_LAG, CHIP_LAG, SHARE_LAG = 3, 1, 4, 6
 
 MESH = pl.DeviceIdType.MESH
 f32 = jnp.float32

time: 97 us -> 94.9 us (0.978)
  Pallas kernels: 91.3 us -> 89.6 us
    pallas_call x1, Pallas kernels: 91.3 us -> 89.6 us  [body(): pl.pallas_call(functools.partial(kernel, sizes), out_shape=[jax.ShapeDtyp...]
where the time goes in v1:
time: 94.9 us; the launch traced here: 94.6 us
  Pallas kernels  89.6 us (94%)
  local copies, waits for them, and re-layouts  4.36 us (5%)
    pallas_call x1, Pallas kernels, body(): pl.pallas_call(functools.partial(kernel, sizes), out_shape=[jax.ShapeDtyp...  89.6 us
    unnamed x2, local copies, waits for them, and re-layouts  4.36 us

profile of v1, /device:TPU:0, one launch (start us, length us, event | category | flops | bytes accessed | tf_op | source)
XLA Modules:
  0.0 94.6 jit_solution(14301443077874610208)
XLA Ops:
  0.6 89.6 %shard_map.50 = (f32[5,40,1024]{2,1,0:T(8,128)}, f32[5,40,1280]{2,1,0:T(8,128)}) custom-call(s32[1024,1280]{1,0:T(8,128)} %counts_ref.1, f32[5,40,1024]{2,1,0:T(8,128)} %bitcast.11, f32[5,40,1280]{2,1,0:T(8,128)} %bitcast.9), custom_call_target="tpu_custom_call" | custom-call | tf_op jit(solution)/shard_map/pallas_call | solution.py:413
  90.2 2.1 %copy.7 = f32[1024,200]{0,1:T(8,128)} copy(f32[1024,200]{0,1:T(8,128)} %bitcast.10) | data formatting | bytes 1638400
  92.3 2.2 %copy.8 = f32[200,1280]{1,0:T(8,128)} copy(f32[200,1280]{1,0:T(8,128)} %bitcast.8) | data formatting | bytes 2048000

commit v2 on v1

--- a/solution.py
+++ b/solution.py
@@ -10,8 +10,9 @@
 ITERS = 2
 LANES = 128
 WIDE = 2 * LANES
-HOP = 4
-GRAM_LAG, CORE_LAG, CHIP_LAG, SHARE_LAG = 3, 1, 4, 6
+HOP, PACE = 8, 2
+GRAM_LAG, CORE_LAG, CHIP_LAG, SHARE_LAG = 7, 3, 13, 16
+JOIN_LAG, SETTLE_LAG = 8, 6
 
 MESH = pl.DeviceIdType.MESH
 f32 = jnp.float32
@@ -53,9 +54,10 @@
     sizes,
     counts_ref, u_ref, p_ref, u_out, p_out,
     counts, e_ref,
-    u_buf, p_buf, zp, z_in, z_out, z_mid, z_fin, g_own, g_all, gram,
-    c_send, c_in, x_buf, x_fin, u_gram,
-    zs_sem, zr_sem, gs_sem, gr_sem, cs_sem, cr_sem, xs_sem, xr_sem, fs_sem, fr_sem, in_sem,
+    u_buf, p_buf, zp, z_in, z_out, z_mid, z_fin, g_own, g_all, gram, below,
+    c_send, c_in, x_buf, x_fin, last_gram, u_gram,
+    zs_sem, zr_sem, gs_sem, gr_sem, cs_sem, cr_sem, xs_sem, xr_sem, fs_sem, fr_sem, ds_sem, dr_sem,
+    in_sem, start_sem, u_sem, p_sem,
 ):
     n_gene, n_cell, n, rows, cells, genes, real_genes, n_slots = sizes
     k = n * rows
@@ -63,8 +65,10 @@
     subs = cells // WIDE
     half_genes = genes // 2
     blocks = gram_blocks(n, rows)
-    lead = 2 * subs
+    lead_chunk = -(-(n - 1) // subs)
+    lead = lead_chunk * subs
     n_pieces = n * subs + n_slots
+    final = n - 1
 
     z = lax.axis_index("gene")
     cell = lax.axis_index("cell")
@@ -81,8 +85,12 @@
         at_row = pl.ds(pl.multiple_of(s * WIDE, WIDE), WIDE)
         return pltpu.make_async_copy(counts_ref.at[at_row], counts.at[s], in_sem.at[s])
 
+    load_program = pltpu.make_async_copy(p_ref, p_buf.at[0], start_sem.at[0])
+    load_usage = pltpu.make_async_copy(u_ref, u_buf.at[0], start_sem.at[1])
+    load_program.start()
     for s in range(subs):
         load(s).start()
+    load_usage.start()
 
     barrier = pltpu.get_barrier_semaphore()
     pl.semaphore_signal(barrier, inc=1, device_id={"gene": inner}, device_id_type=MESH)
@@ -94,10 +102,6 @@
     for away in range(1, n_cell):
         peer = lax.rem(cell + away, n_cell)
         pl.semaphore_signal(barrier, inc=1, device_id={"cell": peer}, device_id_type=MESH)
-    pl.semaphore_wait(barrier, n_cell + 1 - jnp.where(edge, 1, 0))
-
-    u_buf[0] = u_ref[...]
-    p_buf[0] = p_ref[...]
 
     def take_counts(s):
         load(s).wait()
@@ -106,6 +110,16 @@
         if real_genes < genes:
             e_ref[at_row, real_genes:] = jnp.zeros((WIDE, genes - real_genes), jnp.bfloat16)
 
+    def clear(i, carry):
+        u_buf[1 + i // n, lax.rem(i, n)] = jnp.zeros((rows, cells), f32)
+        return carry
+
+    lax.fori_loop(0, ITERS * n, clear, 0)
+    load_program.wait()
+    early = min(2, subs)
+    lax.fori_loop(0, early, lambda s, carry: (take_counts(s), carry)[1], 0)
+    pl.semaphore_wait(barrier, n_cell + 1 - jnp.where(edge, 1, 0))
+
     def remote(src, dst, send, recv, to):
         return pltpu.make_async_remote_copy(
             src_ref=src, dst_ref=dst, send_sem=send, recv_sem=recv, device_id=to, device_id_type=MESH
@@ -130,24 +144,45 @@
         theirs = g_all.at[it, s * n_cell + to]
         return remote(theirs, theirs, gs_sem.at[it, s, away - 1], gr_sem.at[it, s, away - 1], {"cell": to})
 
-    def to_core(it, j):
+    def direct(it, away):
+        to = lax.rem(cell + away, n_cell)
+        mine = last_gram.at[it, cell]
+        return remote(mine, mine, ds_sem.at[it, away - 1], dr_sem.at[it, away - 1], {"cell": to})
+
+    def direct_from(it, away):
+        to = lax.rem(cell + n_cell - away, n_cell)
+        theirs = last_gram.at[it, to]
+        return remote(theirs, theirs, ds_sem.at[it, away - 1], dr_sem.at[it, away - 1], {"cell": to})
+
+    def columns(last):
+        return pl.ds(0, half_genes if last else half_genes + LANES)
+
+    def to_core(it, j, last):
+        at = columns(last)
         return remote(
-            c_send.at[it, j, other], c_in.at[it, j], cs_sem.at[it, j], cr_sem.at[it, j], {"cell": chip * 2 + other}
+            c_send.at[it, j, other, :, at], c_in.at[it, j, :, at], cs_sem.at[it, j], cr_sem.at[it, j],
+            {"cell": chip * 2 + other},
         )
 
-    def to_chip(it, j, away):
+    def to_chip(it, j, away, last):
         to = lax.rem(chip + away, n_chip)
-        mine = x_buf.at[it, j, chip]
+        mine = x_buf.at[it, j, chip, :, columns(last)]
         return remote(mine, mine, xs_sem.at[it, j, away - 1], xr_sem.at[it, j, away - 1], {"cell": to * 2 + core})
 
-    def from_chip(it, j, away):
+    def from_chip(it, j, away, last):
         to = lax.rem(chip + n_chip - away, n_chip)
-        theirs = x_buf.at[it, j, to]
+        theirs = x_buf.at[it, j, to, :, columns(last)]
         return remote(theirs, theirs, xs_sem.at[it, j, away - 1], xr_sem.at[it, j, away - 1], {"cell": to * 2 + core})
 
-    def share(it, j, which):
-        piece = x_fin.at[it, j, which]
+    def share(it, j, which, last):
+        piece = x_fin.at[it, j, which, :, columns(last)]
         return remote(piece, piece, fs_sem.at[it, j], fr_sem.at[it, j], {"cell": chip * 2 + other})
+
+    def put_usage(j):
+        return pltpu.make_async_copy(u_buf.at[ITERS, j], u_out.at[j], u_sem.at[j])
+
+    def put_program(j):
+        return pltpu.make_async_copy(p_buf.at[ITERS, j], p_out.at[j], p_sem.at[j])
 
     def gather_in(it, c):
         @pl.when(edge)
@@ -228,25 +263,73 @@
         for r in range(n):
             gram[r] = full[r * rows:(r + 1) * rows]
 
-    def update_usage(it, j):
-        first = j * subs + jnp.where(j >= 2, n_slots, 0)
+    def usage_below(it, j):
+        below[j] = dot_three(gram[j][:, :k], u_buf[it].reshape(k, cells), 0)
+
+    def update_usage(it, j, last):
+        first = j * subs + jnp.where(j >= lead_chunk, n_slots, 0)
         top = jnp.concatenate([z_fin[it, first + s] for s in range(subs)], 1)
-        old = u_buf[it].reshape(k, cells)
-        new = u_buf[it, j] * top / dot_three(gram[j][:, :k], old, 0)
+        new = u_buf[it, j] * top / below[j]
         u_buf[it + 1, j] = new
+
+        @pl.when(it == ITERS - 1)
+        def _():
+            put_usage(j).start()
 
         def half(h):
             at = pl.ds(pl.multiple_of(h * half_genes, LANES), half_genes)
             c_send[it, j, h, :, :half_genes] = dot_exact_right(new, e_ref[:, at], 0)
 
         own = dot_three(new, u_buf[it + 1].reshape(k, cells), 1)
-        c_send[it, j, 0, :, half_genes:] = own[:, :LANES]
-        c_send[it, j, 1, :, half_genes:] = jnp.concatenate(
-            [own[:, LANES:], jnp.zeros((rows, 2 * LANES - k), f32)], 1
-        )
+        pad = jnp.zeros((rows, 2 * LANES - k), f32)
+        if last:
+            last_gram[it, cell] = jnp.concatenate([own, pad], 1)
+            for away in range(1, n_cell):
+                direct(it, away).start()
+        else:
+            c_send[it, j, 0, :, half_genes:] = own[:, :LANES]
+            c_send[it, j, 1, :, half_genes:] = jnp.concatenate([own[:, LANES:], pad], 1)
         half(other)
-        to_core(it, j).start()
+        to_core(it, j, last).start()
         half(core)
+
+    def join_core(it, j, last):
+        at = columns(last)
+        to_core(it, j, last).wait_recv()
+        x_buf[it, j, chip, :, at] = c_send[it, j, core, :, at] + c_in[it, j, :, at]
+        for away in range(1, n_chip):
+            to_chip(it, j, away, last).start()
+
+    def join_chip(it, j, last):
+        at = columns(last)
+        for away in range(1, n_chip):
+            from_chip(it, j, away, last).wait_recv()
+        total = x_buf[it, j, 0, :, at]
+        for peer in range(1, n_chip):
+            total = total + x_buf[it, j, peer, :, at]
+        x_fin[it, j, core, :, at] = total
+        share(it, j, core, last).start()
+
+    def join_share(it, j, last):
+        share(it, j, other, last).wait_recv()
+
+    def join_usage_gram(it):
+        for away in range(1, n_cell):
+            direct_from(it, away).wait_recv()
+        ending = last_gram[it, 0]
+        for peer in range(1, n_cell):
+            ending = ending + last_gram[it, peer]
+        at_column = lax.broadcasted_iota(jnp.int32, (rows, 2 * LANES), 1)
+        lower, strict = [], []
+        for r in range(n):
+            if r == final:
+                block = ending
+            else:
+                block = jnp.concatenate([x_fin[it, r, h, :, half_genes:] for h in range(2)], 1)
+            lower.append(jnp.where(at_column < (r + 1) * rows, block, 0.0))
+            strict.append(jnp.where(at_column < r * rows, block, 0.0))
+        pad = jnp.zeros((2 * LANES - k, 2 * LANES), f32)
+        u_gram[...] = jnp.concatenate(lower + [pad], 0) + jnp.concatenate(strict + [pad], 0).T
 
     def update_program(it, j):
         top = jnp.concatenate([x_fin[it, j, h, :, :half_genes] for h in range(2)], 1)
@@ -256,7 +339,11 @@
         if real_genes < genes:
             inside = lax.broadcasted_iota(jnp.int32, (rows, genes), 1) < real_genes
             new = jnp.where(inside, new, 0.0)
-        return new
+        p_buf[it + 1, j] = new
+
+        @pl.when(it == ITERS - 1)
+        def _():
+            put_program(j).start()
 
     def settle_pieces(it):
         def pieces(c, carry):
@@ -273,122 +360,110 @@
             for away in range(1, n_cell):
                 spread(it, s, away).wait_send()
 
-    turns = [
-        max((j + 1) * subs + (n_slots if j >= 2 else 0) - 1, lead + n_slots + GRAM_LAG + 2 * j) for j in range(n)
-    ]
-    program_turns = [j * lead // n for j in range(n)]
-
-    def step(it, carry):
-        u_buf[it + 1] = jnp.zeros(u_buf.shape[1:], f32)
-        inward_lag = (reach - 1 - far) * HOP
-        done = (reach + far) * HOP
-        ticks = (2 * reach - 1) * HOP + turns[-1] + SHARE_LAG + 1
-
-        def tick(t, carry):
-            def at(lag, count, act):
-                @pl.when(jnp.logical_and(t >= lag, t < lag + count))
-                def _():
-                    act(t - lag)
-
-            def at_turn(since, when, act):
-                hit, j = since == when[0], 0
-                for i in range(1, n):
-                    now = since == when[i]
-                    hit, j = jnp.logical_or(hit, now), jnp.where(now, i, j)
-
-                @pl.when(hit)
-                def _():
-                    act(j)
-
-            def next_program(j):
-                p_buf[it, j] = update_program(it - 1, j)
-
-            @pl.when(jnp.logical_and(it == 0, t < subs))
+    def settle_chunks(it):
+        def chunks(j, last):
+            to_core(it, j, last).wait_send()
+            for away in range(1, n_chip):
+                to_chip(it, j, away, last).wait_send()
+            share(it, j, core, last).wait_send()
+
+        lax.fori_loop(0, final, lambda j, carry: (chunks(j, False), carry)[1], 0)
+        chunks(final, True)
+        for away in range(1, n_cell):
+            direct(it, away).wait_send()
+
+    place = [(j + 1) * subs - 1 + (n_slots if j >= lead_chunk else 0) for j in range(n)]
+    gram_place = PACE * (lead + n_slots - 1)
+    joined = gram_place + GRAM_LAG
+    turns = [max(PACE * place[j], joined + 1 + 2 * j) for j in range(n)]
+    below_turns = [joined + 2 * j for j in range(n)]
+    inward_lag = (reach - 1 - far) * HOP
+    done = (reach + far) * HOP
+    period = (2 * reach - 1) * HOP + turns[final] + JOIN_LAG
+    ticks = ITERS * period + n
+    pace_in = jnp.where(edge, 1, PACE)
+
+    def tick(t, carry):
+        def frame(start):
+            it = 0
+            for i in range(1, ITERS):
+                it = it + jnp.where(t >= start + i * period, 1, 0)
+            return it, t - start - it * period
+
+        def at_turn(start, when, act):
+            it, since = frame(start)
+            hit, j = since == when[0], 0
+            for i in range(1, len(when)):
+                now = since == when[i]
+                hit, j = jnp.logical_or(hit, now), jnp.where(now, i, j)
+
+            @pl.when(hit)
             def _():
-                take_counts(t)
-
-            at_turn(jnp.where(it > 0, t, -1), program_turns, next_program)
-            q = t - jnp.where(t >= lead + n_slots, n_slots, 0)
-            a_piece = jnp.logical_and(jnp.logical_or(t < lead, t >= lead + n_slots), q < n * subs)
-
-            @pl.when(a_piece)
+                act(it, j)
+
+        def at_chunk(start, when, lag, last_lag, act):
+            at_turn(start + lag, when[:final], lambda it, j: act(it, j, False))
+            at_turn(start + last_lag, when[final:], lambda it, j: act(it, final, True))
+
+        def at_time(start, act):
+            at_turn(start, [0], lambda it, j: act(it))
+
+        @pl.when(jnp.logical_and(t >= early, t < subs))
+        def _():
+            take_counts(t)
+
+        at_chunk(done, turns, CORE_LAG, CORE_LAG, join_core)
+        at_chunk(done, turns, CHIP_LAG, JOIN_LAG + 2, join_chip)
+        at_chunk(done, turns, SHARE_LAG, JOIN_LAG + final, join_share)
+        at_time(period, join_usage_gram)
+        at_turn(period, list(range(n)), update_program)
+
+        it, since = frame(0)
+        q = since - jnp.where(since >= lead + n_slots, n_slots, 0)
+
+        @pl.when(jnp.logical_and(jnp.logical_or(since < lead, since >= lead + n_slots), q < n * subs))
+        def _():
+            numerator(it, q)
+
+        @pl.when(since == lead)
+        def _():
+            own_gram(it)
+
+        def at_pieces(start, pace, act):
+            it, since = frame(start)
+            c = since // pace
+
+            @pl.when(jnp.logical_and(jnp.logical_and(since >= 0, c * pace == since), c < n_pieces))
             def _():
-                numerator(it, q)
-
-            @pl.when(t == lead)
-            def _():
-                own_gram(it)
-
-            at(inward_lag, n_pieces, lambda c: gather_in(it, c))
-            at(done, n_pieces, lambda c: spread_out(it, c))
-
-            @pl.when(t == done + lead + n_slots - 1)
-            def _():
-                spread_gram(it)
-
-            @pl.when(t == done + lead + n_slots + GRAM_LAG)
-            def _():
-                join_gram(it)
-
-            at_turn(t - done, turns, lambda j: update_usage(it, j))
-
-            def join_core(j):
-                to_core(it, j).wait_recv()
-                x_buf[it, j, chip] = c_send[it, j, core] + c_in[it, j]
-                for away in range(1, n_chip):
-                    to_chip(it, j, away).start()
-
-            at_turn(t - done - CORE_LAG, turns, join_core)
-
-            @pl.when(t == done + CORE_LAG + turns[-1])
-            def _():
-                settle_pieces(it)
-            def join_chip(j):
-                for away in range(1, n_chip):
-                    from_chip(it, j, away).wait_recv()
-                total = x_buf[it, j, 0]
-                for peer in range(1, n_chip):
-                    total = total + x_buf[it, j, peer]
-                x_fin[it, j, core] = total
-                share(it, j, core).start()
-
-            at_turn(t - done - CHIP_LAG, turns, join_chip)
-            at_turn(t - done - SHARE_LAG, turns, lambda j: share(it, j, other).wait_recv())
-            return carry
-
-        lax.fori_loop(0, ticks, tick, 0)
-
-        columns = lax.broadcasted_iota(jnp.int32, (rows, 2 * LANES), 1)
-        lower, strict = [], []
-        for r in range(n):
-            block = jnp.concatenate([x_fin[it, r, h, :, half_genes:] for h in range(2)], 1)
-            lower.append(jnp.where(columns < (r + 1) * rows, block, 0.0))
-            strict.append(jnp.where(columns < r * rows, block, 0.0))
-        pad = jnp.zeros((2 * LANES - k, 2 * LANES), f32)
-        u_gram[...] = jnp.concatenate(lower + [pad], 0) + jnp.concatenate(strict + [pad], 0).T
+                act(it, c)
+
+        it_in, since_in = frame(inward_lag)
+        c_in_turn = jnp.where(edge, since_in, since_in // PACE)
+
+        @pl.when(
+            jnp.logical_and(
+                jnp.logical_and(since_in >= 0, c_in_turn * pace_in == since_in), c_in_turn < n_pieces
+            )
+        )
+        def _():
+            gather_in(it_in, c_in_turn)
+
+        at_pieces(done, PACE, spread_out)
+        at_time(done + gram_place, spread_gram)
+        at_time(done + joined, join_gram)
+        at_turn(done, below_turns, usage_below)
+        at_chunk(done, turns, 0, 0, update_usage)
+        at_time(done + turns[final] + SETTLE_LAG, settle_pieces)
         return carry
 
-    lax.fori_loop(0, ITERS, step, 0)
-
-    def last_program(j, carry):
-        p_out[j] = update_program(ITERS - 1, j)
-        return carry
-
-    lax.fori_loop(0, n, last_program, 0)
-    u_out[...] = u_buf[ITERS]
-
-    def settle(it, carry):
-        def chunks(j, carry):
-            to_core(it, j).wait_send()
-            for away in range(1, n_chip):
-                to_chip(it, j, away).wait_send()
-            share(it, j, core).wait_send()
-            return carry
-
-        lax.fori_loop(0, n, chunks, 0)
-        return carry
-
-    lax.fori_loop(0, ITERS, settle, 0)
+    load_usage.wait()
+    lax.fori_loop(0, ticks, tick, 0)
+
+    for it in range(ITERS):
+        settle_chunks(it)
+    for j in range(n):
+        put_usage(j).wait()
+        put_program(j).wait()
 
 
 def body(mesh, counts, usage_init, program_init):
@@ -408,7 +483,7 @@
         program = jnp.pad(program, ((0, 0), (0, genes - real_genes)))
 
     sizes = (n_gene, n_cell, n, rows, cells, genes, real_genes, n_slots)
-    vmem = pl.BlockSpec(memory_space=pltpu.VMEM)
+    anywhere = pl.BlockSpec(memory_space=pl.ANY)
     dma = pltpu.SemaphoreType.DMA
     usage, program = pl.pallas_call(
         functools.partial(kernel, sizes),
@@ -416,8 +491,8 @@
             jax.ShapeDtypeStruct((n, rows, cells), f32),
             jax.ShapeDtypeStruct((n, rows, genes), f32),
         ],
-        in_specs=[pl.BlockSpec(memory_space=pl.ANY), vmem, vmem],
-        out_specs=[vmem] * 2,
+        in_specs=[anywhere] * 3,
+        out_specs=[anywhere] * 2,
         scratch_shapes=[
             pltpu.VMEM((cells // WIDE, WIDE, real_genes), jnp.int32),
             pltpu.VMEM((cells, genes), jnp.bfloat16),
@@ -431,10 +506,12 @@
             pltpu.VMEM((n_slots * n_cell, rows, WIDE), f32),
             pltpu.VMEM((ITERS, n_slots * n_cell, rows, WIDE), f32),
             pltpu.VMEM((n, rows, 2 * LANES), f32),
+            pltpu.VMEM((n, rows, cells), f32),
             pltpu.VMEM((ITERS, n, 2, rows, width), f32),
             pltpu.VMEM((ITERS, n, rows, width), f32),
             pltpu.VMEM((ITERS, n, n_chip, rows, width), f32),
             pltpu.VMEM((ITERS, n, 2, rows, width), f32),
+            pltpu.VMEM((ITERS, n_cell, rows, 2 * LANES), f32),
             pltpu.VMEM((2 * LANES, 2 * LANES), f32),
             dma((ITERS, 2, n_pieces)),
             dma((ITERS, 2, n_pieces)),
@@ -446,7 +523,12 @@
             dma((ITERS, n, max(n_chip - 1, 1))),
             dma((ITERS, n)),
             dma((ITERS, n)),
+            dma((ITERS, n_cell - 1)),
+            dma((ITERS, n_cell - 1)),
             dma((cells // WIDE,)),
+            dma((2,)),
+            dma((n,)),
+            dma((n,)),
         ],
         compiler_params=pltpu.CompilerParams(
             collective_id=0, has_side_effects=True, vmem_limit_bytes=60 * 1024 * 1024

time: 94.9 us -> 97.8 us (1.031)
  Pallas kernels: 89.6 us -> 92.6 us
    pallas_call x1, Pallas kernels: 89.6 us -> 92.6 us  [body(): pl.pallas_call(functools.partial(kernel, sizes), out_shape=[jax.ShapeDtyp...]
where the time goes in v2:
time: 97.8 us; the launch traced here: 97.6 us
  Pallas kernels  92.6 us (95%)
  local copies, waits for them, and re-layouts  4.36 us (4%)
    pallas_call x1, Pallas kernels, body(): pl.pallas_call(functools.partial(kernel, sizes), out_shape=[jax.ShapeDtyp...  92.6 us
    unnamed x2, local copies, waits for them, and re-layouts  4.36 us

profile of v2, /device:TPU:0, one launch (start us, length us, event | category | flops | bytes accessed | tf_op | source)
XLA Modules:
  0.0 97.6 jit_solution(15755893423836500595)
XLA Ops:
  0.6 92.6 %shard_map.50 = (f32[5,40,1024]{2,1,0:T(8,128)}, f32[5,40,1280]{2,1,0:T(8,128)}) custom-call(s32[1024,1280]{1,0:T(8,128)} %counts_ref.1, f32[5,40,1024]{2,1,0:T(8,128)} %bitcast.11, f32[5,40,1280]{2,1,0:T(8,128)} %bitcast.9), custom_call_target="tpu_custom_call" | custom-call | tf_op jit(solution)/shard_map/pallas_call | solution.py:488
  93.3 2.1 %copy.7 = f32[1024,200]{0,1:T(8,128)} copy(f32[1024,200]{0,1:T(8,128)} %bitcast.10) | data formatting | bytes 1638400
  95.4 2.2 %copy.8 = f32[200,1280]{1,0:T(8,128)} copy(f32[200,1280]{1,0:T(8,128)} %bitcast.8) | data formatting | bytes 2048000

commit v3 on v2

--- a/solution.py
+++ b/solution.py
@@ -10,9 +10,9 @@
 ITERS = 2
 LANES = 128
 WIDE = 2 * LANES
-HOP, PACE = 8, 2
-GRAM_LAG, CORE_LAG, CHIP_LAG, SHARE_LAG = 7, 3, 13, 16
-JOIN_LAG, SETTLE_LAG = 8, 6
+HOP, PACE = 4, 1
+GRAM_LAG, CORE_LAG, CHIP_LAG, SHARE_LAG = 5, 2, 7, 9
+JOIN_LAG, SETTLE_LAG = 5, 4
 
 MESH = pl.DeviceIdType.MESH
 f32 = jnp.float32

time: 97.8 us -> 89.5 us (0.915)
  Pallas kernels: 92.6 us -> 84.3 us
    pallas_call x1, Pallas kernels: 92.6 us -> 84.3 us  [body(): pl.pallas_call(functools.partial(kernel, sizes), out_shape=[jax.ShapeDtyp...]
where the time goes in v3:
time: 89.5 us; the launch traced here: 89.3 us
  Pallas kernels  84.3 us (94%)
  local copies, waits for them, and re-layouts  4.36 us (5%)
    pallas_call x1, Pallas kernels, body(): pl.pallas_call(functools.partial(kernel, sizes), out_shape=[jax.ShapeDtyp...  84.3 us
    unnamed x2, local copies, waits for them, and re-layouts  4.36 us

profile of v3, /device:TPU:0, one launch (start us, length us, event | category | flops | bytes accessed | tf_op | source)
XLA Modules:
  0.0 89.3 jit_solution(11708194935614236499)
XLA Ops:
  0.6 84.3 %shard_map.50 = (f32[5,40,1024]{2,1,0:T(8,128)}, f32[5,40,1280]{2,1,0:T(8,128)}) custom-call(s32[1024,1280]{1,0:T(8,128)} %counts_ref.1, f32[5,40,1024]{2,1,0:T(8,128)} %bitcast.11, f32[5,40,1280]{2,1,0:T(8,128)} %bitcast.9), custom_call_target="tpu_custom_call" | custom-call | tf_op jit(solution)/shard_map/pallas_call | solution.py:488
  84.9 2.1 %copy.7 = f32[1024,200]{0,1:T(8,128)} copy(f32[1024,200]{0,1:T(8,128)} %bitcast.10) | data formatting | bytes 1638400
  87.0 2.2 %copy.8 = f32[200,1280]{1,0:T(8,128)} copy(f32[200,1280]{1,0:T(8,128)} %bitcast.8) | data formatting | bytes 2048000

commit v4 on v3

--- a/solution.py
+++ b/solution.py
@@ -11,7 +11,7 @@
 LANES = 128
 WIDE = 2 * LANES
 HOP, PACE = 4, 1
-GRAM_LAG, CORE_LAG, CHIP_LAG, SHARE_LAG = 5, 2, 7, 9
+GRAM_LAG, CORE_LAG, CHIP_LAG, SHARE_LAG = 4, 2, 7, 9
 JOIN_LAG, SETTLE_LAG = 5, 4
 
 MESH = pl.DeviceIdType.MESH
@@ -412,11 +412,17 @@
         def _():
             take_counts(t)
 
-        at_chunk(done, turns, CORE_LAG, CORE_LAG, join_core)
-        at_chunk(done, turns, CHIP_LAG, JOIN_LAG + 2, join_chip)
-        at_chunk(done, turns, SHARE_LAG, JOIN_LAG + final, join_share)
-        at_time(period, join_usage_gram)
-        at_turn(period, list(range(n)), update_program)
+        turn = frame(done)[1]
+        opening = frame(period)[1]
+
+        @pl.when(turn >= turns[0] + SHARE_LAG)
+        def _():
+            at_chunk(done, turns, SHARE_LAG, JOIN_LAG + final, join_share)
+
+        @pl.when(jnp.logical_and(opening >= 0, opening < n))
+        def _():
+            at_time(period, join_usage_gram)
+            at_turn(period, list(range(n)), update_program)
 
         it, since = frame(0)
         q = since - jnp.where(since >= lead + n_slots, n_slots, 0)
@@ -449,11 +455,20 @@
             gather_in(it_in, c_in_turn)
 
         at_pieces(done, PACE, spread_out)
-        at_time(done + gram_place, spread_gram)
-        at_time(done + joined, join_gram)
-        at_turn(done, below_turns, usage_below)
-        at_chunk(done, turns, 0, 0, update_usage)
-        at_time(done + turns[final] + SETTLE_LAG, settle_pieces)
+
+        @pl.when(turn >= turns[0] + CORE_LAG)
+        def _():
+            at_chunk(done, turns, CORE_LAG, CORE_LAG, join_core)
+            at_chunk(done, turns, CHIP_LAG, JOIN_LAG + 2, join_chip)
+
+        @pl.when(turn >= gram_place)
+        def _():
+            at_time(done + gram_place, spread_gram)
+            at_time(done + joined, join_gram)
+            at_turn(done, below_turns, usage_below)
+            at_chunk(done, turns, 0, 0, update_usage)
+            at_time(done + turns[final] + SETTLE_LAG, settle_pieces)
+
         return carry
 
     load_usage.wait()
@@ -464,6 +479,18 @@
     for j in range(n):
         put_usage(j).wait()
         put_program(j).wait()
+
+
+def hand_over(n, u_ref, p_ref, u_out, p_out, sem):
+    moves = [
+        pltpu.make_async_copy(src.at[j], dst.at[j], sem.at[i, j])
+        for i, (src, dst) in enumerate([(p_ref, p_out), (u_ref, u_out)])
+        for j in range(n)
+    ]
+    for move in moves:
+        move.start()
+    for move in moves:
+        move.wait()
 
 
 def body(mesh, counts, usage_init, program_init):
@@ -484,6 +511,7 @@
 
     sizes = (n_gene, n_cell, n, rows, cells, genes, real_genes, n_slots)
     anywhere = pl.BlockSpec(memory_space=pl.ANY)
+    in_hbm = pl.BlockSpec(memory_space=pltpu.HBM)
     dma = pltpu.SemaphoreType.DMA
     usage, program = pl.pallas_call(
         functools.partial(kernel, sizes),
@@ -491,7 +519,7 @@
             jax.ShapeDtypeStruct((n, rows, cells), f32),
             jax.ShapeDtypeStruct((n, rows, genes), f32),
         ],
-        in_specs=[anywhere] * 3,
+        in_specs=[in_hbm] * 3,
         out_specs=[anywhere] * 2,
         scratch_shapes=[
             pltpu.VMEM((cells // WIDE, WIDE, real_genes), jnp.int32),
@@ -531,13 +559,24 @@
             dma((n,)),
         ],
         compiler_params=pltpu.CompilerParams(
-            collective_id=0, has_side_effects=True, vmem_limit_bytes=60 * 1024 * 1024
+            collective_id=0, has_side_effects=True, vmem_limit_bytes=48 * 1024 * 1024
         ),
     )(
         counts,
         usage_init.T.reshape(n, rows, cells),
         program.reshape(n, rows, genes),
     )
+    usage, program = pl.pallas_call(
+        functools.partial(hand_over, n),
+        out_shape=[
+            jax.ShapeDtypeStruct((n, rows, cells), f32),
+            jax.ShapeDtypeStruct((n, rows, genes), f32),
+        ],
+        in_specs=[anywhere] * 2,
+        out_specs=[in_hbm] * 2,
+        scratch_shapes=[dma((2, n))],
+        compiler_params=pltpu.CompilerParams(vmem_limit_bytes=1024 * 1024),
+    )(usage, program)
     usage = usage.reshape(k, cells).T
     program = program.reshape(k, genes)[:, :real_genes]
     return usage, program

time: 89.5 us -> 86.9 us (0.971)
  local copies, waits for them, and re-layouts: 4.36 us -> 2.35 us
    unnamed x2 -> x4, local copies, waits for them, and re-layouts: 4.36 us -> 2.35 us
    pallas_call x1, Pallas kernels: 84.3 us -> 82.4 us  [body(): pl.pallas_call(functools.partial(kernel, sizes), out_shape=[jax.ShapeDtyp...]
    pallas_call x0 -> x1, Pallas kernels: none -> 1.31 us  [body(): pl.pallas_call(functools.partial(hand_over, n), out_shape=[jax.ShapeDtype...]
where the time goes in v4:
time: 86.9 us; the launch traced here: 86.7 us
  Pallas kernels  83.7 us (96%)
  local copies, waits for them, and re-layouts  2.35 us (3%)
    pallas_call x1, Pallas kernels, body(): pl.pallas_call(functools.partial(kernel, sizes), out_shape=[jax.ShapeDtyp...  82.4 us
    unnamed x4, local copies, waits for them, and re-layouts  2.35 us

profile of v4, /device:TPU:0, one launch (start us, length us, event | category | flops | bytes accessed | tf_op | source)
XLA Modules:
  0.0 86.7 jit_solution(12303308440547572331)
XLA Ops:
  0.6 0.0 copy-start
  0.6 1.2 %copy-done = f32[200,1280]{1,0:T(8,128)S(1)} copy-done((f32[200,1280]{1,0:T(8,128)S(1)}, f32[200,1280]{1,0:T(8,128)}, u32[]{:S(2)}) %copy-start) | copy-done | bytes 1024024
  1.8 0.0 copy-start.1
  1.8 1.1 %copy-done.1 = f32[1024,200]{0,1:T(8,128)S(1)} copy-done((f32[1024,200]{0,1:T(8,128)S(1)}, f32[1024,200]{0,1:T(8,128)}, u32[]{:S(2)}) %copy-start.1) | copy-done | bytes 819224
  3.0 82.4 %shard_map.50 = (f32[5,40,1024]{2,1,0:T(8,128)S(1)}, f32[5,40,1280]{2,1,0:T(8,128)S(1)}) custom-call(s32[1024,1280]{1,0:T(8,128)} %counts_ref.1, f32[5,40,1024]{2,1,0:T(8,128)S(1)} %bitcast.9, f32[5,40,1280]{2,1,0:T(8,128)S(1)} %bitcast.8), custom_call_target="tpu_custom_call" | custom-call | tf_op jit(solution)/shard_map/pallas_call | solution.py:516
  85.4 1.3 %shard_map.51 = (f32[5,40,1024]{2,1,0:T(8,128)}, f32[5,40,1280]{2,1,0:T(8,128)}) custom-call(f32[5,40,1024]{2,1,0:T(8,128)S(1)} %get-tuple-element.6.u_ref, f32[5,40,1280]{2,1,0:T(8,128)S(1)} %get-tuple-element.7.p_ref), custom_call_target="tpu_custom_call" | custom-call | tf_op jit(solution)/shard_map/pallas_call | solution.py:569
Async XLA Ops:
  0.6 1.2 %copy-start = (f32[200,1280]{1,0:T(8,128)S(1)}, f32[200,1280]{1,0:T(8,128)}, u32[]{:S(2)}) copy-start(f32[200,1280]{1,0:T(8,128)} %param.5) | copy-start | bytes 3072004
  1.8 1.1 %copy-start.1 = (f32[1024,200]{0,1:T(8,128)S(1)}, f32[1024,200]{0,1:T(8,128)}, u32[]{:S(2)}) copy-start(f32[1024,200]{0,1:T(8,128)} %param.4) | copy-start | bytes 2457604
